TPU v7x, 32 devices: a whole 2x2x4 slice. The times are simulated.
32 devices in a mesh: frame: 16 (over z, y, x), head: 2 (over core).
Axes of the slice: x: 2, y: 2, z: 4, core: 2. Of those that a mesh axis runs over, the one named last changes fastest.
Arguments:
- residual: bfloat16 [2048, 5120], P('frame', 'head'), may hold values from -48 to 48
- query_proj: bfloat16 [2048, 3072], P('frame', 'head'), may hold values from -200 to 200
- key_proj: bfloat16 [2048, 3072], P('frame', 'head'), may hold values from -200 to 200
- value_proj: bfloat16 [2048, 3072], P('frame', 'head'), may hold values from -6 to 6
- q_gain: float32 [3072], P('head'), may hold values from 1 to 3
- k_gain: float32 [3072], P('head'), may hold values from 1 to 3
- time_embed: float32 [5120], P(('frame', 'head')), may hold values from -6 to 6
- time_proj: bfloat16 [5120, 3, 5120], P(('frame', 'head')), may hold values from -0.15625 to 0.15625
- mod_table: float32 [3, 5120], P(None, 'head'), may hold values from -3 to 3
- out_weight: bfloat16 [3072, 5120], P('head'), may hold values from -0.109375 to 0.109375
Outputs:
- hidden_out: bfloat16 [2048, 5120], P('frame', 'head')
- mlp_input: bfloat16 [2048, 5120], P('frame', 'head')
All inputs are finite; a program needn't handle non-finite values.
Results may differ from a plain program's by a relative error of at most 0.0071.
Values may be sent and summed in bfloat16 or wider, within the bound.
A program may use at most 128 MiB of HBM per device.

v0:
```python
import math
import jax
import jax.numpy as jnp
from jax import lax
from jax.sharding import PartitionSpec as P

D = 5120
HEADS = 24
HD = 128


def accumulate(carry, queries, keys_block, values_block):
    count = keys_block.shape[0]
    heads_here = queries.shape[1]
    keys_three = keys_block.reshape(count, heads_here, HD)
    values_three = values_block.reshape(count, heads_here, HD).astype(jnp.float32)
    scores = jnp.einsum("thd,shd->ths", queries, keys_three, preferred_element_type=jnp.float32) * (
        1.0 / math.sqrt(HD)
    )
    top_old, total_old, summed = carry
    top_new = jnp.maximum(top_old, jnp.max(scores, axis=2))
    weights = jnp.exp(scores - top_new[:, :, None])
    total_new = jnp.sum(weights, axis=2)
    summed_new = jnp.einsum("ths,shd->thd", weights, values_three, precision=lax.Precision.HIGHEST)
    return (top_new, total_new, summed_new)


def shards(
    residual,
    query_proj,
    key_proj,
    value_proj,
    q_gain,
    k_gain,
    time_embed,
    time_proj,
    mod_table,
    out_weight,
):
    emb = jax.nn.silu(time_embed)
    partial_mod = jnp.einsum(
        "r,rcd->cd", emb, time_proj.astype(jnp.float32), precision=lax.Precision.HIGHEST
    )
    width = mod_table.shape[1]
    summed_mod = lax.psum(partial_mod, ("frame", "head"))
    share = lax.dynamic_slice_in_dim(summed_mod, lax.axis_index("head") * width, width, 1)
    modulation = mod_table + share
    gate = modulation[0]
    shift = modulation[1]
    scale = modulation[2]
    tok_rows = query_proj.shape[0]
    heads_here = query_proj.shape[1] // HD
    query_wide = query_proj.astype(jnp.float32)
    key_wide = key_proj.astype(jnp.float32)
    total_q, total_k = lax.psum(
        (jnp.sum(query_wide * query_wide, axis=1), jnp.sum(key_wide * key_wide, axis=1)), "head"
    )
    query_rms = lax.rsqrt(total_q / (HEADS * HD) + 1e-06)
    key_rms = lax.rsqrt(total_k / (HEADS * HD) + 1e-06)
    queries = (
        (query_wide * query_rms[:, None] * q_gain)
        .astype(jnp.bfloat16)
        .reshape(tok_rows, heads_here, HD)
    )
    start_state = (
        jnp.full((tok_rows, heads_here), -1e30, jnp.float32),
        jnp.zeros((tok_rows, heads_here), jnp.float32),
        jnp.zeros((tok_rows, heads_here, HD), jnp.float32),
    )
    every_scale = lax.all_gather(key_rms, "frame", axis=0, tiled=True)
    keys_block = (
        lax.all_gather(key_proj, "frame", axis=0, tiled=True).astype(jnp.float32)
        * every_scale[:, None]
        * k_gain
    ).astype(jnp.bfloat16)
    top_final, total_final, summed_final = accumulate(
        start_state, queries, keys_block, lax.all_gather(value_proj, "frame", axis=0, tiled=True)
    )
    attn = (
        (summed_final / total_final[:, :, None])
        .astype(jnp.bfloat16)
        .reshape(tok_rows, heads_here * HD)
    )
    proj = (
        lax.psum_scatter(
            lax.dot_general(
                out_weight, attn, (((0,), (1,)), ((), ())), preferred_element_type=jnp.float32
            ).astype(jnp.bfloat16),
            "head",
            scatter_dimension=0,
            tiled=True,
        )
        .astype(jnp.float32)
        .T
    )
    hidden_out = (residual.astype(jnp.float32) + gate * proj).astype(jnp.bfloat16)
    hidden32 = lax.optimization_barrier(hidden_out).astype(jnp.float32)
    row_sum, row_squares = lax.psum(
        (jnp.sum(hidden32, axis=1), jnp.sum(hidden32 * hidden32, axis=1)), "head"
    )
    mean = row_sum[:, None] / D
    var = row_squares[:, None] / D - mean * mean
    mlp_input = ((hidden32 - mean) * lax.rsqrt(var + 1e-06) * (1.0 + scale) + shift).astype(
        jnp.bfloat16
    )
    return (hidden_out, mlp_input)


def solution(mesh):
    in_specs = (
        P("frame", "head"),
        P("frame", "head"),
        P("frame", "head"),
        P("frame", "head"),
        P("head"),
        P("head"),
        P(("frame", "head")),
        P(("frame", "head"), None, None),
        P(None, "head"),
        P("head", None),
    )
    out_specs = (P("frame", "head"), P("frame", "head"))
    return jax.shard_map(shards, mesh=mesh, in_specs=in_specs, out_specs=out_specs, check_vma=False)
```

profile of v0, /device:TPU:0, one launch (start us, length us, event | category | flops | bytes accessed | tf_op | source)
XLA Modules:
  0.0 312.0 jit_solution(16471371955343777573)
XLA Ops:
  7.2 0.0 all-gather.4.cloned.1.call-start
  7.2 1.9 copy.22
  9.1 0.0 all-gather.4.cloned.1.call-update
  9.1 0.0 all-gather.6.cloned.1.call-start
  9.2 0.7 all-gather.6.cloned.1.call-update
  9.9 0.0 reduce-scatter.2.cloned.1.call-start
  9.9 1.2 copy.23
  11.2 1.2 multiply_reduce_fusion
  12.3 0.2 fusion.22
  12.6 2.6 all-reduce.1
  15.2 42.8 %all-gather = f32[16,1,128]{2,1,0:T(1,128)S(1)} all-gather(f32[1,1,128]{2,1,0:T(1,128)S(1)} %rsqrt_bitcast_fusion), channel_id=1, replica_groups=mesh['frame'=16,'head'=2] {'frame'}, dimensions={0}, use_global_device_ids=true | all-gather | bytes 8704 | tf_op jit(solution)/shard_map/all_gather | solution.py:70
  58.0 1.0 fusion.24
  59.0 70.0 %all-gather.4.cloned.1.call-done = bf16[2048,1536]{0,1:T(8,128)(2,1)} async-done(((bf16[128,1536]{0,1:T(8,128)(2,1)}), bf16[2048,1536]{0,1:T(8,128)(2,1)}) %all-gather.4.cloned.1.call-update) | async-done | bytes 6291472 | tf_op jit(solution)/shard_map/all_gather | solution.py:72
  129.0 6.9 %multiply_convert_fusion = bf16[2048,1536]{0,1:T(8,128)(2,1)} fusion(bf16[2048,1536]{0,1:T(8,128)(2,1)} %all-gather.4.cloned.1.call-done, f32[1536]{0:T(1024)} %param.15, f32[2048]{0:T(1024)S(1)} %bitcast.49), kind=kLoop, calls=%fused_computation.3 | loop fusion | flops 12582912 | bytes 12597248 | tf_op jit(solution)/shard_map/convert_element_type | solution.py:75
  135.9 4.7 %bitcast_reduce_fusion = (f32[128,12]{0,1:T(8,128)S(1)}, f32[12,2048,128]{2,1,0:T(8,128)S(1)}) fusion(bf16[2048,12,128]{0,2,1:T(8,128)(2,1)} %bitcast.44, bf16[128,12,128]{0,2,1:T(8,128)(2,1)S(1)} %bitcast.46), kind=kOutput, calls=%fused_computation.1 | convolution fusion | flops 811596288 | bytes 19273728 | tf_op jit(solution)/shard_map/thd,shd->ths/dot_general | solution.py:17
  140.6 0.0 copy-start
  140.6 4.5 %copy-done = f32[12,2048,128]{2,1,0:T(8,128)} copy-done((f32[12,2048,128]{2,1,0:T(8,128)}, f32[12,2048,128]{2,1,0:T(8,128)S(1)}, u32[]{:S(2)}) %copy-start) | copy-done | bytes 12582936
  145.2 2.1 fusion.1
  147.3 76.2 %all-gather.6.cloned.1.call-done = bf16[2048,1536]{1,0:T(8,128)(2,1)} async-done(((bf16[128,1536]{1,0:T(8,128)(2,1)}), bf16[2048,1536]{1,0:T(8,128)(2,1)}) %all-gather.6.cloned.1.call-update) | async-done | bytes 6291472 | tf_op jit(solution)/shard_map/all_gather | solution.py:77
  223.4 8.7 %copy.26 = bf16[2048,1536]{0,1:T(8,128)(2,1)} copy(bf16[2048,1536]{1,0:T(8,128)(2,1)} %all-gather.6.cloned.1.call-done) | data formatting | bytes 12582912 | tf_op jit(solution)/shard_map/all_gather | solution.py:77
  232.1 14.6 %fusion.19 = bf16[128,12,128]{0,2,1:T(8,128)(2,1)S(1)} fusion(bf16[2048,12,128]{0,2,1:T(8,128)(2,1)} %bitcast.45, f32[12,2048,128]{2,1,0:T(8,128)} %copy-done, f32[128,12]{0,1:T(8,128)S(1)} %broadcast_maximum_fusion, f32[128,12]{0,1:T(8,128)S(1)} %fusion.1), kind=kOutput, calls=%fused_computation.24 | convolution fusion | flops 4838522880 | bytes 19279872 | tf_op jit(solution)/shard_map/ths,shd->thd/dot_general | solution.py:24
  246.8 0.0 copy-start.4
  246.8 8.8 %fusion.6 = bf16[5120,128]{0,1:T(8,128)(2,1)} fusion(bf16[128,1536]{0,1:T(8,128)(2,1)S(1)} %bitcast.47, bf16[1536,5120]{1,0:T(8,128)(2,1)} %param.19), kind=kOutput, calls=%fused_computation.9 | convolution fusion | flops 2013921280 | bytes 17432576 | tf_op jit(solution)/shard_map/dot_general | solution.py:86
  255.6 0.0 copy-start.3
  255.6 0.0 copy-start.2
  255.6 0.0 reduce-scatter.2.cloned.1.call-update
  255.6 0.0 copy-done.4
  255.7 4.7 %fusion.27 = f32[1,3,5120]{2,0,1:T(1,128)S(1)} fusion(f32[160,1,1]{0,1,2:T(1,128)S(1)} %bitcast.50, bf16[160,3,5120]{2,0,1:T(8,128)(2,1)} %param.17), kind=kOutput, calls=%fused_computation.42 | convolution fusion | flops 29491200 | bytes 4977280 | tf_op jit(solution)/shard_map/r,rcd->cd/dot_general | solution.py:41
  260.4 39.6 %psum.35 = f32[3,5120]{1,0:T(4,128)S(1)} all-reduce(f32[3,5120]{1,0:T(4,128)S(1)} %bitcast.48), channel_id=1, replica_groups=mesh['frame'=16,'head'=2] {'frame','head'}, use_global_device_ids=true, to_apply=%region_0.1 | all-reduce | flops 15360 | bytes 122880 | tf_op jit(solution)/shard_map/psum | solution.py:45
  300.0 0.0 copy-done.3
  300.0 0.1 fusion.25
  300.1 0.0 reduce-scatter.2.cloned.1.call-done
  300.1 0.0 copy-done.2
  300.1 1.3 fusion.12
  301.4 0.0 copy-start.1
  301.4 0.3 convert_reduce_fusion
  301.7 2.5 all-reduce
  304.2 1.3 fusion.10
  305.5 0.0 copy-done.1
  (7 shorter events, 0.1 us)
Async XLA Ops:
  7.2 121.9 %all-gather.4.cloned.1.call-start = ((), (), s32[]{:S(2)}) async-start(), calls=%async_computation.1 | async-start | bytes 6684672 | tf_op jit(solution)/shard_map/all_gather | solution.py:72
  9.1 214.3 %all-gather.6.cloned.1.call-start = ((), (), s32[]{:S(2)}) async-start(), calls=%async_computation.2 | async-start | bytes 6684672 | tf_op jit(solution)/shard_map/all_gather | solution.py:77
  9.9 290.2 %reduce-scatter.2.cloned.1.call-start = ((), (), s32[]{:S(2)}) async-start(), calls=%async_computation.3 | async-start | bytes 1966080 | tf_op jit(solution)/shard_map/reduce_scatter | solution.py:85
  140.6 4.6 %copy-start = (f32[12,2048,128]{2,1,0:T(8,128)}, f32[12,2048,128]{2,1,0:T(8,128)S(1)}, u32[]{:S(2)}) copy-start(f32[12,2048,128]{2,1,0:T(8,128)S(1)} %get-tuple-element.14) | copy-start | bytes 37748740
  246.8 8.9 %copy-start.4 = (f32[160]{0:T(256)S(1)}, f32[160]{0:T(256)}, u32[]{:S(2)}) copy-start(f32[160]{0:T(256)} %param.16) | copy-start | bytes 1924
  255.6 44.4 %copy-start.3 = (f32[3,2560]{1,0:T(4,128)S(1)}, f32[3,2560]{1,0:T(4,128)}, u32[]{:S(2)}) copy-start(f32[3,2560]{1,0:T(4,128)} %param.18) | copy-start | bytes 92164
  255.6 44.5 %copy-start.2 = (bf16[128,2560]{1,0:T(8,128)(2,1)S(1)}, bf16[128,2560]{1,0:T(8,128)(2,1)}, u32[]{:S(2)}) copy-start(bf16[128,2560]{1,0:T(8,128)(2,1)} %param.10) | copy-start | bytes 1966084
  301.4 4.1 %copy-start.1 = (bf16[128,2560]{1,0:T(8,128)(2,1)}, bf16[128,2560]{1,0:T(8,128)(2,1)S(1)}, u32[]{:S(2)}) copy-start(bf16[128,2560]{1,0:T(8,128)(2,1)S(1)} %fusion.12) | copy-start | bytes 1966084
Sparse Core Ops, SparseCore 0:
  11.2 117.7 all-gather.3
  131.8 91.5 all-gather.5
  255.7 7.1 reduce-scatter.1
where the time goes:
time: 313 us; the launch traced here: 312 us
  waiting for transfers between devices  147 us (47%)
  blocking collectives  87.5 us (28%)
  matrix products  32.8 us (10%)
  local copies, waits for them, and re-layouts  16.4 us (5%)
  other arithmetic  14.3 us (5%)
  between operations  13.9 us (4%)
    all_gather x1, waiting for transfers between devices, shards(): lax.all_gather(value_proj, 'frame', axis=0, tiled=True)  76.2 us
    all_gather x1, waiting for transfers between devices, shards(): lax.all_gather(key_proj, 'frame', axis=0, tiled=True).astype(jnp.float32)  70 us
    all_gather x1, blocking collectives, shards(): every_scale = lax.all_gather(key_rms, 'frame', axis=0, tiled=True)  42.8 us
    psum x1, blocking collectives, shards(): summed_mod = lax.psum(partial_mod, ('frame', 'head'))  39.6 us
    dot_general x1, matrix products, accumulate(): jnp.einsum('ths,shd->thd', weights, values_three, precision=lax.Precision...  14.6 us
    dot_general x1, matrix products, shards(): lax.dot_general(out_weight, attn, (((0,), (1,)), ((), ())), preferred_ele...  8.81 us
    all_gather x1, local copies, waits for them, and re-layouts, shards(): lax.all_gather(value_proj, 'frame', axis=0, tiled=True)  8.7 us
    unnamed x12, local copies, waits for them, and re-layouts  7.7 us
  transfers between devices with their start and end apart: 3, of which 2 were waited for; matrix products, arithmetic and copies ran while one was open for 7% of the time, Pallas kernels for 0%

commit v1 on v0

--- a/solution.py
+++ b/solution.py
@@ -42,7 +42,7 @@
         "r,rcd->cd", emb, time_proj.astype(jnp.float32), precision=lax.Precision.HIGHEST
     )
     width = mod_table.shape[1]
-    summed_mod = lax.psum(partial_mod, ("frame", "head"))
+    summed_mod = jnp.sum(lax.all_gather(partial_mod, ("frame", "head")), axis=0)
     share = lax.dynamic_slice_in_dim(summed_mod, lax.axis_index("head") * width, width, 1)
     modulation = mod_table + share
     gate = modulation[0]

time: 313 us -> 305 us (0.974)
  blocking collectives: 87.5 us -> 48 us
  waiting for transfers between devices: 147 us -> 180 us
    psum x1 -> x0, blocking collectives: 39.6 us -> none  [shards(): summed_mod = lax.psum(partial_mod, ('frame', 'head'))]
    all_gather x0 -> x1, waiting for transfers between devices: none -> 17.7 us  [shards(): summed_mod = jnp.sum(lax.all_gather(partial_mod, ('frame', 'head')), axis=0)]
    all_gather x1, waiting for transfers between devices: 76.2 us -> 87.5 us  [shards(): lax.all_gather(value_proj, 'frame', axis=0, tiled=True)]
    reduce_scatter x1, waiting for transfers between devices: 0.02 us -> 7.32 us  [shards(): lax.psum_scatter(lax.dot_general(out_weight, attn, (((0,), (1,)), ((), ()...]
    all_gather x1, waiting for transfers between devices: 70 us -> 66.8 us  [shards(): lax.all_gather(key_proj, 'frame', axis=0, tiled=True).astype(jnp.float32)]
    unnamed x12 -> x18, local copies, waits for them, and re-layouts: 7.7 us -> 4.71 us
  transfers between devices with their start and end apart: 3 -> 4, of which waited for: 2 -> 4; matrix products, arithmetic and copies ran while one was open for 7% -> 18% of each run, Pallas kernels for 0% -> 0%
where the time goes in v1:
time: 305 us
  waiting for transfers between devices  180 us (59%)
  blocking collectives  48 us (16%)
  matrix products  33.1 us (11%)
  other arithmetic  15.4 us (5%)
  local copies, waits for them, and re-layouts  14 us (5%)
  between operations  13.9 us (5%)
    all_gather x1, waiting for transfers between devices, shards(): lax.all_gather(value_proj, 'frame', axis=0, tiled=True)  87.5 us
    all_gather x1, waiting for transfers between devices, shards(): lax.all_gather(key_proj, 'frame', axis=0, tiled=True).astype(jnp.float32)  66.8 us
    all_gather x1, blocking collectives, shards(): every_scale = lax.all_gather(key_rms, 'frame', axis=0, tiled=True)  42.9 us
    all_gather x1, waiting for transfers between devices, shards(): summed_mod = jnp.sum(lax.all_gather(partial_mod, ('frame', 'head')), axis=0)  17.7 us
    dot_general x1, matrix products, accumulate(): jnp.einsum('ths,shd->thd', weights, values_three, precision=lax.Precision...  14.7 us
    dot_general x1, matrix products, shards(): lax.dot_general(out_weight, attn, (((0,), (1,)), ((), ())), preferred_ele...  9.14 us
    all_gather x1, local copies, waits for them, and re-layouts, shards(): lax.all_gather(value_proj, 'frame', axis=0, tiled=True)  8.62 us
    reduce_scatter x1, waiting for transfers between devices, shards(): lax.psum_scatter(lax.dot_general(out_weight, attn, (((0,), (1,)), ((), ()...  7.32 us
  transfers between devices with their start and end apart: 4, of which 4 were waited for; matrix products, arithmetic and copies ran while one was open for 18% of the time, Pallas kernels for 0%

profile of v1, /device:TPU:0, one launch (start us, length us, event | category | flops | bytes accessed | tf_op | source)
XLA Modules:
  0.0 304.6 jit_solution(2561973870683443484)
XLA Ops:
  7.2 0.0 copy-start.2
  7.2 0.0 copy-start.4
  7.2 0.0 copy-start.6
  7.2 0.0 copy-start.7
  7.2 0.0 all-gather.7.cloned.1.call-start
  7.3 2.0 copy.22
  9.2 0.0 all-gather.7.cloned.1.call-update
  9.2 0.0 all-gather.9.cloned.1.call-start
  9.3 0.7 all-gather.9.cloned.1.call-update
  10.0 0.0 all-gather.11.cloned.1.call-start
  10.0 0.7 divide_multiply_fusion
  10.7 4.4 %fusion.27 = f32[1,3,5120]{2,0,1:T(1,128)S(1)} fusion(f32[160,1,1]{0,1,2:T(1,128)S(1)} %bitcast.47, bf16[160,3,5120]{2,0,1:T(8,128)(2,1)} %param.17), kind=kOutput, calls=%fused_computation.41 | convolution fusion | flops 29491200 | bytes 4977280 | tf_op jit(solution)/shard_map/r,rcd->cd/dot_general | solution.py:41
  15.1 0.7 copy.28
  15.8 0.0 all-gather.11.cloned.1.call-update
  15.8 0.0 reduce-scatter.2.cloned.1.call-start
  15.9 0.0 copy-done.2
  15.9 0.2 multiply_reduce_fusion
  16.1 0.0 copy-done.4
  16.1 0.2 copy.23
  16.3 0.2 fusion.22
  16.5 2.6 all-reduce.1
  19.1 42.9 %all-gather.2 = f32[16,1,128]{2,1,0:T(1,128)S(1)} all-gather(f32[1,1,128]{2,1,0:T(1,128)S(1)} %rsqrt_bitcast_fusion), channel_id=1, replica_groups=mesh['frame'=16,'head'=2] {'frame'}, dimensions={0}, use_global_device_ids=true | all-gather | bytes 8704 | tf_op jit(solution)/shard_map/all_gather | solution.py:70
  62.0 0.0 copy-done.6
  62.0 0.3 fusion.24
  62.3 66.8 %all-gather.7.cloned.1.call-done = bf16[2048,1536]{0,1:T(8,128)(2,1)} async-done(((bf16[128,1536]{0,1:T(8,128)(2,1)}), bf16[2048,1536]{0,1:T(8,128)(2,1)}) %all-gather.7.cloned.1.call-update) | async-done | bytes 6291472 | tf_op jit(solution)/shard_map/all_gather | solution.py:72
  129.1 0.0 copy-done.7
  129.1 6.8 %multiply_convert_fusion = bf16[2048,1536]{0,1:T(8,128)(2,1)} fusion(bf16[2048,1536]{0,1:T(8,128)(2,1)} %all-gather.7.cloned.1.call-done, f32[1536]{0:T(1024)S(1)} %copy-done.7, f32[2048]{0:T(1024)S(1)} %bitcast.46), kind=kLoop, calls=%fused_computation.3 | loop fusion | flops 12582912 | bytes 12597248 | tf_op jit(solution)/shard_map/convert_element_type | solution.py:75
  135.9 87.5 %all-gather.9.cloned.1.call-done = bf16[2048,1536]{1,0:T(8,128)(2,1)} async-done(((bf16[128,1536]{1,0:T(8,128)(2,1)}), bf16[2048,1536]{1,0:T(8,128)(2,1)}) %all-gather.9.cloned.1.call-update) | async-done | bytes 6291472 | tf_op jit(solution)/shard_map/all_gather | solution.py:77
  223.5 8.6 %copy.26 = bf16[2048,1536]{0,1:T(8,128)(2,1)} copy(bf16[2048,1536]{1,0:T(8,128)(2,1)} %all-gather.9.cloned.1.call-done) | data formatting | bytes 12582912 | tf_op jit(solution)/shard_map/all_gather | solution.py:77
  232.1 4.9 %bitcast_reduce_fusion = (f32[128,12]{0,1:T(8,128)S(1)}, f32[12,2048,128]{2,1,0:T(8,128)S(1)}) fusion(bf16[2048,12,128]{0,2,1:T(8,128)(2,1)} %bitcast.42, bf16[128,12,128]{0,2,1:T(8,128)(2,1)S(1)} %bitcast.44), kind=kOutput, calls=%fused_computation.1 | convolution fusion | flops 811596288 | bytes 19273728 | tf_op jit(solution)/shard_map/thd,shd->ths/dot_general | solution.py:17
  237.0 0.0 copy-start
  237.0 2.1 fusion.1
  239.1 2.5 copy-done
  241.6 14.7 %fusion.19 = bf16[128,12,128]{0,2,1:T(8,128)(2,1)S(1)} fusion(bf16[2048,12,128]{0,2,1:T(8,128)(2,1)} %bitcast.43, f32[12,2048,128]{2,1,0:T(8,128)} %copy-done, f32[128,12]{0,1:T(8,128)S(1)} %broadcast_maximum_fusion, f32[128,12]{0,1:T(8,128)S(1)} %fusion.1), kind=kOutput, calls=%fused_computation.24 | convolution fusion | flops 4838522880 | bytes 19279872 | tf_op jit(solution)/shard_map/ths,shd->thd/dot_general | solution.py:24
  256.2 0.0 copy-start.5
  256.2 0.0 copy-start.3
  256.2 9.1 %fusion.6 = bf16[5120,128]{0,1:T(8,128)(2,1)} fusion(bf16[128,1536]{0,1:T(8,128)(2,1)S(1)} %bitcast.45, bf16[1536,5120]{1,0:T(8,128)(2,1)} %param.19), kind=kOutput, calls=%fused_computation.9 | convolution fusion | flops 2013921280 | bytes 17432576 | tf_op jit(solution)/shard_map/dot_general | solution.py:86
  265.4 0.0 reduce-scatter.2.cloned.1.call-update
  265.4 17.7 %all-gather.11.cloned.1.call-done = f32[32,3,5120]{2,1,0:T(4,128)} async-done(((f32[1,3,5120]{2,1,0:T(4,128)}), f32[32,3,5120]{2,1,0:T(4,128)}) %all-gather.11.cloned.1.call-update) | async-done | bytes 1966096 | tf_op jit(solution)/shard_map/all_gather | solution.py:45
  283.1 2.1 reduce_sum.54
  285.3 0.1 fusion.25
  285.4 7.3 %reduce-scatter.2.cloned.1.call-done = bf16[2560,128]{0,1:T(8,128)(2,1)} async-done(((bf16[5120,128]{0,1:T(8,128)(2,1)}), bf16[2560,128]{0,1:T(8,128)(2,1)}) %reduce-scatter.2.cloned.1.call-update) | async-done | bytes 655376 | tf_op jit(solution)/shard_map/reduce_scatter | solution.py:85
  292.7 0.0 copy-done.3
  292.7 1.3 fusion.12
  294.0 0.0 copy-start.1
  294.0 0.3 convert_reduce_fusion
  294.2 2.5 all-reduce
  296.7 1.3 fusion.10
  (7 shorter events, 0.0 us)
Async XLA Ops:
  7.2 8.7 %copy-start.2 = (bf16[128,1536]{1,0:T(8,128)(2,1)S(1)}, bf16[128,1536]{1,0:T(8,128)(2,1)}, u32[]{:S(2)}) copy-start(bf16[128,1536]{1,0:T(8,128)(2,1)} %param.12) | copy-start | bytes 1179652
  7.2 8.9 %copy-start.4 = (bf16[128,1536]{1,0:T(8,128)(2,1)S(1)}, bf16[128,1536]{1,0:T(8,128)(2,1)}, u32[]{:S(2)}) copy-start(bf16[128,1536]{1,0:T(8,128)(2,1)} %param.11) | copy-start | bytes 1179652
  7.2 54.8 %copy-start.6 = (f32[1536]{0:T(1024)S(1)}, f32[1536]{0:T(1024)}, u32[]{:S(2)}) copy-start(f32[1536]{0:T(1024)} %param.14) | copy-start | bytes 18436
  7.2 121.9 %copy-start.7 = (f32[1536]{0:T(1024)S(1)}, f32[1536]{0:T(1024)}, u32[]{:S(2)}) copy-start(f32[1536]{0:T(1024)} %param.15) | copy-start | bytes 18436
  7.2 121.9 %all-gather.7.cloned.1.call-start = ((), (), s32[]{:S(2)}) async-start(), calls=%async_computation.1 | async-start | bytes 6684672 | tf_op jit(solution)/shard_map/all_gather | solution.py:72
  9.2 214.2 %all-gather.9.cloned.1.call-start = ((), (), s32[]{:S(2)}) async-start(), calls=%async_computation.2 | async-start | bytes 6684672 | tf_op jit(solution)/shard_map/all_gather | solution.py:77
  10.0 273.1 %all-gather.11.cloned.1.call-start = ((), (), s32[]{:S(2)}) async-start(), calls=%async_computation.4 | async-start | bytes 2703360 | tf_op jit(solution)/shard_map/all_gather | solution.py:45
  15.8 276.9 %reduce-scatter.2.cloned.1.call-start = ((), (), s32[]{:S(2)}) async-start(), calls=%async_computation.3 | async-start | bytes 1966080 | tf_op jit(solution)/shard_map/reduce_scatter | solution.py:85
  237.0 4.6 %copy-start = (f32[12,2048,128]{2,1,0:T(8,128)}, f32[12,2048,128]{2,1,0:T(8,128)S(1)}, u32[]{:S(2)}) copy-start(f32[12,2048,128]{2,1,0:T(8,128)S(1)} %get-tuple-element.14) | copy-start | bytes 37748740
  256.2 29.0 %copy-start.5 = (f32[3,2560]{1,0:T(4,128)S(1)}, f32[3,2560]{1,0:T(4,128)}, u32[]{:S(2)}) copy-start(f32[3,2560]{1,0:T(4,128)} %param.18) | copy-start | bytes 92164
  256.2 36.5 %copy-start.3 = (bf16[128,2560]{1,0:T(8,128)(2,1)S(1)}, bf16[128,2560]{1,0:T(8,128)(2,1)}, u32[]{:S(2)}) copy-start(bf16[128,2560]{1,0:T(8,128)(2,1)} %param.10) | copy-start | bytes 1966084
  294.0 4.1 %copy-start.1 = (bf16[128,2560]{1,0:T(8,128)(2,1)}, bf16[128,2560]{1,0:T(8,128)(2,1)S(1)}, u32[]{:S(2)}) copy-start(bf16[128,2560]{1,0:T(8,128)(2,1)S(1)} %fusion.12) | copy-start | bytes 1966084
Sparse Core Ops, SparseCore 0:
  11.3 117.7 all-gather.6
  131.9 91.5 all-gather.8
  226.9 56.1 all-gather.10
  285.2 7.4 reduce-scatter.1
